TPU v7x, 32 devices: a whole 2x2x4 slice. The times are simulated.
32 devices in a mesh: dom: 4 (over y, x), fsdp: 8 (over z, core).
Axes of the slice: x: 2, y: 2, z: 4, core: 2. Of those that a mesh axis runs over, the one named last changes fastest.
Arguments:
- inputs: bfloat16 [4, 1024, 4096], P('dom', 'fsdp'), may hold values from -6 to 6
- cotangent: bfloat16 [4, 1024, 8192], P('dom', 'fsdp'), may hold values from -6 to 6
- shared_weight: bfloat16 [4096, 8192], P(None, 'fsdp'), may hold values from -0.09375 to 0.09375
- domain_weight: bfloat16 [4, 4096, 8192], P('dom', None, 'fsdp'), may hold values from 0.099609375 to 1.8984375
- row_counts: int32 [4], P('dom'), may hold values from 65 to 1024, as said below
Outputs:
- shared_grad: float32 [4096, 8192], P('dom', 'fsdp')
- domain_grad: bfloat16 [4, 4096, 8192], P('dom', None, 'fsdp')
- input_grad: bfloat16 [4, 1024, 4096], P('dom', 'fsdp')
Inputs may be any that keep to these rules, and one draw needn't show every extreme that they name: `row_counts`: rows of a domain at positions from its count on are padding. Some domain is full in every draw.
All inputs are finite; a program needn't handle non-finite values.
Results may differ from a plain program's by a relative error of at most 0.017.
Values may be sent and summed in bfloat16 or wider, within the bound.
A program may use at most 128 MiB of HBM per device.

v0:
```python
import jax
import jax.numpy as jnp
from jax import lax
from jax.sharding import PartitionSpec as P


def body(inputs, cotangent, shared_weight, domain_weight, row_counts):
    effective = (shared_weight.astype(jnp.float32) * domain_weight[0].astype(jnp.float32)).astype(
        jnp.bfloat16
    )
    live_rows = row_counts[0]
    columns = lax.all_to_all(cotangent[0], "fsdp", split_axis=1, concat_axis=0, tiled=True)
    piece = lax.all_gather(inputs[0], "fsdp", axis=0, tiled=True)
    length = piece.shape[0]
    upstream = columns.astype(jnp.float32)
    preact = jnp.dot(piece, effective, preferred_element_type=jnp.float32)
    sigma = jax.nn.sigmoid(preact)
    position = lax.iota(jnp.int32, length)
    slope = upstream * sigma * (1.0 + preact * (1.0 - sigma))
    fold_grad_pre = jnp.where((position < live_rows)[:, None], slope, jnp.float32(0.0)).astype(
        jnp.bfloat16
    )
    weight_sum = lax.dot_general(
        piece, fold_grad_pre, (((0,), (0,)), ((), ())), preferred_element_type=jnp.float32
    )
    weight_sum, grad_pre = (weight_sum, fold_grad_pre)
    scaled = weight_sum * lax.rsqrt(live_rows.astype(jnp.float32))
    input_grad = lax.psum_scatter(
        lax.dot_general(
            grad_pre, effective, (((1,), (1,)), ((), ())), preferred_element_type=jnp.float32
        ).astype(jnp.bfloat16),
        "fsdp",
        scatter_dimension=0,
        tiled=True,
    )
    shared_grad = lax.psum_scatter(
        (scaled * domain_weight[0].astype(jnp.float32)).astype(jnp.bfloat16),
        "dom",
        scatter_dimension=0,
        tiled=True,
    ).astype(jnp.float32)
    domain_grad = (scaled * shared_weight.astype(jnp.float32)).astype(jnp.bfloat16)
    return (shared_grad, domain_grad[None], input_grad[None])


def solution(mesh):
    return jax.shard_map(
        body,
        mesh=mesh,
        in_specs=(
            P("dom", "fsdp", None),
            P("dom", "fsdp", None),
            P(None, "fsdp"),
            P("dom", None, "fsdp"),
            P("dom"),
        ),
        out_specs=(P("dom", "fsdp"), P("dom", None, "fsdp"), P("dom", "fsdp", None)),
        check_vma=False,
    )
```

profile of v0, /device:TPU:0, one launch (start us, length us, event | category | flops | bytes accessed | tf_op | source)
XLA Modules:
  0.0 358.8 jit_solution(8678285528174618740)
XLA Ops:
  7.2 0.0 all-gather.3.cloned.1.call-start
  7.2 0.7 all-gather.3.cloned.1.call-update
  7.9 4.1 %copy.13 = bf16[1,128,8192]{1,2,0:T(8,128)(2,1)} copy(bf16[1,128,8192]{2,1,0:T(8,128)(2,1)} %param.6) | data formatting | bytes 4194304 | tf_op args[1]
  12.0 6.4 %all-to-all-start = ((bf16[128,8,1024]{0,2,1:T(8,128)(2,1)}), bf16[128,8,1024]{0,2,1:T(8,128)(2,1)S(1)}, u32[]{:S(2)}, u32[]{:S(2)}) async-start(bf16[128,8,1024]{0,2,1:T(8,128)(2,1)} %bitcast.1), calls=%async_computation | async-start | bytes 4194304 | tf_op jit(solution)/shard_map/all_to_all | solution.py:12
  18.3 0.0 reduce-scatter.3.cloned.1.call-start
  19.1 11.3 %copy.15 = bf16[4096,1024]{0,1:T(8,128)(2,1)} copy(bf16[4096,1024]{1,0:T(8,128)(2,1)} %param.7) | data formatting | bytes 16777216 | tf_op args[2]
  30.4 11.3 %copy.16 = bf16[1,4096,1024]{1,2,0:T(8,128)(2,1)} copy(bf16[1,4096,1024]{2,1,0:T(8,128)(2,1)} %param.8) | data formatting | bytes 16777216 | tf_op args[3]
  41.6 81.1 %all-to-all-done = bf16[128,8,1024]{0,2,1:T(8,128)(2,1)S(1)} async-done(((bf16[128,8,1024]{0,2,1:T(8,128)(2,1)}), bf16[128,8,1024]{0,2,1:T(8,128)(2,1)S(1)}, u32[]{:S(2)}, u32[]{:S(2)}) %all-to-all-start) | async-done | bytes 2097184 | tf_op jit(solution)/shard_map/all_to_all | solution.py:12
  122.7 13.7 %all-gather.3.cloned.1.call-done = bf16[1,1024,4096]{2,1,0:T(8,128)(2,1)} async-done(((bf16[1,128,4096]{2,1,0:T(8,128)(2,1)}), bf16[1,1024,4096]{2,1,0:T(8,128)(2,1)}) %all-gather.3.cloned.1.call-update) | async-done | bytes 8388624 | tf_op jit(solution)/shard_map/all_gather | solution.py:13
  136.4 17.1 %fusion.10 = bf16[1024,1024]{0,1:T(8,128)(2,1)} fusion(bf16[1,1024,4096]{2,1,0:T(8,128)(2,1)} %all-gather.3.cloned.1.call-done, bf16[4096,1024]{0,1:T(8,128)(2,1)} %copy.15, bf16[1,4096,1024]{1,2,0:T(8,128)(2,1)} %copy.16, pred[1024]{0:T(1024)(128)(4,1)S(1)} %iota_compare_fusion, bf16[128,8,1024]{0,2,1:T(8,128)(2,1)S(1)} %all-to-all-done), kind=kOutput, calls=%fused_computation.15 | convolution fusion | flops 8618246144 | bytes 29361152 | tf_op jit(solution)/shard_map/dot_general | solution.py:16
  153.5 20.9 %fusion.3 = (bf16[1,4096,1024]{1,2,0:T(8,128)(2,1)}, bf16[4096,1024]{0,1:T(8,128)(2,1)}) fusion(bf16[4096,1024]{0,1:T(8,128)(2,1)} %copy.15, f32[]{:T(128)S(6)} %rsqrt.3, bf16[1,4096,1024]{1,2,0:T(8,128)(2,1)} %copy.16, bf16[1024,1024]{0,1:T(8,128)(2,1)} %fusion.10, bf16[1,1024,4096]{2,1,0:T(8,128)(2,1)} %all-gather.3.cloned.1.call-done), kind=kOutput, calls=%fused_computation.6 | convolution fusion | flops 8619294720 | bytes 44040196 | tf_op jit(solution)/shard_map/dot_general | solution.py:23
  174.4 0.0 copy-start
  174.4 0.0 reduce-scatter.3.cloned.1.call-update
  174.5 0.2 reduce-scatter.5.cloned.1.call-start
  174.7 1.3 copy-done
  176.0 17.8 %convolution_convert_fusion = bf16[1024,4096]{1,0:T(8,128)(2,1)} fusion(bf16[1024,1024]{0,1:T(8,128)(2,1)S(1)} %copy-done, bf16[4096,1024]{0,1:T(8,128)(2,1)} %copy.15, bf16[1,4096,1024]{1,2,0:T(8,128)(2,1)} %copy.16), kind=kOutput, calls=%fused_computation.11 | convolution fusion | flops 8610906112 | bytes 27262976 | tf_op jit(solution)/shard_map/dot_general | solution.py:29
  193.8 0.0 reduce-scatter.5.cloned.1.call-update
  193.9 12.0 %copy.18 = bf16[1,4096,1024]{2,1,0:T(8,128)(2,1)} copy(bf16[1,4096,1024]{1,2,0:T(8,128)(2,1)} %get-tuple-element.9) | data formatting | bytes 16777216
  205.9 54.0 %reduce-scatter.3.cloned.1.call-done = bf16[1024,1024]{0,1:T(8,128)(2,1)} async-done(((bf16[4096,1024]{0,1:T(8,128)(2,1)}), bf16[1024,1024]{0,1:T(8,128)(2,1)}) %reduce-scatter.3.cloned.1.call-update) | async-done | bytes 2097168 | tf_op jit(solution)/shard_map/reduce_scatter | solution.py:36
  259.8 4.1 %copy.17 = f32[1024,1024]{1,0:T(8,128)} copy(bf16[1024,1024]{0,1:T(8,128)(2,1)} %reduce-scatter.3.cloned.1.call-done) | data formatting | bytes 6291456
  263.9 88.3 %reduce-scatter.5.cloned.1.call-done = bf16[128,4096]{1,0:T(8,128)(2,1)} async-done(((bf16[1024,4096]{1,0:T(8,128)(2,1)}), bf16[128,4096]{1,0:T(8,128)(2,1)}) %reduce-scatter.5.cloned.1.call-update) | async-done | bytes 1048592 | tf_op jit(solution)/shard_map/reduce_scatter | solution.py:28
  (1 shorter events, 0.0 us)
Async XLA Ops:
  7.2 129.2 %all-gather.3.cloned.1.call-start = ((), (), s32[]{:S(2)}) async-start(), calls=%async_computation.5 | async-start | bytes 9437184 | tf_op jit(solution)/shard_map/all_gather | solution.py:13
  12.0 110.8 %all-to-all-start = ((bf16[128,8,1024]{0,2,1:T(8,128)(2,1)}), bf16[128,8,1024]{0,2,1:T(8,128)(2,1)S(1)}, u32[]{:S(2)}, u32[]{:S(2)}) async-start(bf16[128,8,1024]{0,2,1:T(8,128)(2,1)} %bitcast.1), calls=%async_computation | async-start | bytes 4194304 | tf_op jit(solution)/shard_map/all_to_all | solution.py:12
  18.3 241.5 %reduce-scatter.3.cloned.1.call-start = ((), (), s32[]{:S(2)}) async-start(), calls=%async_computation.3 | async-start | bytes 10485760 | tf_op jit(solution)/shard_map/reduce_scatter | solution.py:36
  174.4 1.6 copy-start
  174.5 177.8 %reduce-scatter.5.cloned.1.call-start = ((), (), s32[]{:S(2)}) async-start(), calls=%async_computation.4 | async-start | bytes 9437184 | tf_op jit(solution)/shard_map/reduce_scatter | solution.py:28
Sparse Core Ops, SparseCore 0:
  9.6 126.7 all-gather.2
  174.6 85.2 reduce-scatter.2
  262.7 89.5 reduce-scatter.4
where the time goes:
time: 360 us; the launch traced here: 359 us
  waiting for transfers between devices  238 us (66%)
  matrix products  55.8 us (16%)
  local copies, waits for them, and re-layouts  44.1 us (12%)
  between operations  14.4 us (4%)
  starting transfers between devices  6.65 us (2%)
    reduce_scatter x1, waiting for transfers between devices, body(): lax.psum_scatter(lax.dot_general(grad_pre, effective, (((1,), (1,)), ((),...  88.3 us
    all_to_all x1, waiting for transfers between devices, body(): lax.all_to_all(cotangent[0], 'fsdp', split_axis=1, concat_axis=0, tiled=T...  81.1 us
    reduce_scatter x1, waiting for transfers between devices, body(): lax.psum_scatter((scaled * domain_weight[0].astype(jnp.float32)).astype(j...  54 us
    unnamed x7, local copies, waits for them, and re-layouts  44.1 us
    dot_general x1, matrix products, body(): lax.dot_general(piece, fold_grad_pre, (((0,), (0,)), ((), ())), preferred...  20.9 us
    dot_general x1, matrix products, body(): lax.dot_general(grad_pre, effective, (((1,), (1,)), ((), ())), preferred_...  17.8 us
    dot_general x1, matrix products, body(): preact = jnp.dot(piece, effective, preferred_element_type=jnp.float32)  17.1 us
    all_gather x1, waiting for transfers between devices, body(): piece = lax.all_gather(inputs[0], 'fsdp', axis=0, tiled=True)  13.7 us
  transfers between devices with their start and end apart: 4, of which 4 were waited for; matrix products, arithmetic and copies ran while one was open for 17% of the time, Pallas kernels for 0%

commit v1 on v0

--- a/solution.py
+++ b/solution.py
@@ -9,7 +9,12 @@
         jnp.bfloat16
     )
     live_rows = row_counts[0]
-    columns = lax.all_to_all(cotangent[0], "fsdp", split_axis=1, concat_axis=0, tiled=True)
+    columns = jnp.concatenate(
+        lax.all_to_all(
+            jnp.stack(jnp.split(cotangent[0], lax.axis_size("fsdp"), axis=1)), "fsdp", 0, 0
+        ),
+        axis=0,
+    )
     piece = lax.all_gather(inputs[0], "fsdp", axis=0, tiled=True)
     length = piece.shape[0]
     upstream = columns.astype(jnp.float32)

time: 360 us -> 363 us (level)
  waiting for transfers between devices: 238 us -> 223 us
  local copies, waits for them, and re-layouts: 44.1 us -> 58.5 us
    all_gather x1, waiting for transfers between devices: 13.7 us -> 1.49 us  [body(): piece = lax.all_gather(inputs[0], 'fsdp', axis=0, tiled=True)]
    unnamed x7 -> x11, local copies, waits for them, and re-layouts: 44.1 us -> 51.4 us
    convert_element_type x0 -> x1, local copies, waits for them, and re-layouts: none -> 5.44 us  [body(): upstream = columns.astype(jnp.float32)]
    all_to_all x1, waiting for transfers between devices: 81.1 us -> 77.5 us  [body(): lax.all_to_all(jnp.stack(jnp.split(cotangent[0], lax.axis_size('fsdp'), a...]
  transfers between devices with their start and end apart: 4 -> 4, of which waited for: 4 -> 4; matrix products, arithmetic and copies ran while one was open for 17% -> 22% of each run, Pallas kernels for 0% -> 0%
where the time goes in v1:
time: 363 us; the launch traced here: 361 us
  waiting for transfers between devices  223 us (61%)
  local copies, waits for them, and re-layouts  58.5 us (16%)
  matrix products  56.4 us (16%)
  between operations  14.4 us (4%)
  starting transfers between devices  6.65 us (2%)
    reduce_scatter x1, waiting for transfers between devices, body(): lax.psum_scatter(lax.dot_general(grad_pre, effective, (((1,), (1,)), ((),...  88.3 us
    all_to_all x1, waiting for transfers between devices, body(): lax.all_to_all(jnp.stack(jnp.split(cotangent[0], lax.axis_size('fsdp'), a...  77.5 us
    reduce_scatter x1, waiting for transfers between devices, body(): lax.psum_scatter((scaled * domain_weight[0].astype(jnp.float32)).astype(j...  54.6 us
    unnamed x11, local copies, waits for them, and re-layouts  51.4 us
    dot_general x1, matrix products, body(): lax.dot_general(piece, fold_grad_pre, (((0,), (0,)), ((), ())), preferred...  19.5 us
    dot_general x1, matrix products, body(): preact = jnp.dot(piece, effective, preferred_element_type=jnp.float32)  19 us
    dot_general x1, matrix products, body(): lax.dot_general(grad_pre, effective, (((1,), (1,)), ((), ())), preferred_...  17.8 us
  transfers between devices with their start and end apart: 4, of which 4 were waited for; matrix products, arithmetic and copies ran while one was open for 22% of the time, Pallas kernels for 0%

profile of v1, /device:TPU:0, one launch (start us, length us, event | category | flops | bytes accessed | tf_op | source)
XLA Modules:
  0.0 361.2 jit_solution(13402438352389351388)
XLA Ops:
  7.2 0.0 all-gather.3.cloned.1.call-start
  7.2 0.7 all-gather.3.cloned.1.call-update
  7.9 1.7 fusion.26
  9.6 1.7 fusion.25
  11.2 1.7 fusion.24
  12.9 1.7 fusion.23
  14.6 1.7 fusion.22
  16.2 1.7 fusion.21
  17.9 1.7 fusion.20
  19.6 1.7 fusion.19
  21.3 6.3 %all-to-all-start = ((bf16[8,128,1024]{2,1,0:T(8,128)(2,1)}), bf16[8,128,1024]{2,1,0:T(8,128)(2,1)S(1)}, u32[]{:S(2)}, u32[]{:S(2)}) async-start(bf16[8,128,1024]{2,1,0:T(8,128)(2,1)} %fusion.19), calls=%async_computation | async-start | bytes 4194304 | tf_op jit(solution)/shard_map/all_to_all | solution.py:13
  27.7 0.0 reduce-scatter.3.cloned.1.call-start
  28.4 11.9 %copy.9 = bf16[4096,1024]{0,1:T(8,128)(2,1)} copy(bf16[4096,1024]{1,0:T(8,128)(2,1)} %param.7) | data formatting | bytes 16777216 | tf_op args[2]
  40.3 11.5 %copy.10 = bf16[1,4096,1024]{1,2,0:T(8,128)(2,1)} copy(bf16[1,4096,1024]{2,1,0:T(8,128)(2,1)} %param.8) | data formatting | bytes 16777216 | tf_op args[3]
  51.9 77.5 %all-to-all-done = bf16[8,128,1024]{2,1,0:T(8,128)(2,1)S(1)} async-done(((bf16[8,128,1024]{2,1,0:T(8,128)(2,1)}), bf16[8,128,1024]{2,1,0:T(8,128)(2,1)S(1)}, u32[]{:S(2)}, u32[]{:S(2)}) %all-to-all-start) | async-done | bytes 2097184 | tf_op jit(solution)/shard_map/all_to_all | solution.py:13
  129.3 2.6 bitcast_convert_fusion
  131.9 5.4 %copy.13 = f32[1024,1024]{0,1:T(8,128)} copy(f32[1024,1024]{1,0:T(8,128)} %bitcast_convert_fusion) | data formatting | bytes 8388608 | tf_op jit(solution)/shard_map/convert_element_type | solution.py:20
  137.4 1.5 all-gather.3.cloned.1.call-done
  138.9 19.0 %fusion.14 = bf16[1024,1024]{0,1:T(8,128)(2,1)S(1)} fusion(f32[1024,1024]{0,1:T(8,128)} %copy.13, bf16[1,1024,4096]{2,1,0:T(8,128)(2,1)} %all-gather.3.cloned.1.call-done, bf16[4096,1024]{0,1:T(8,128)(2,1)} %copy.9, bf16[1,4096,1024]{1,2,0:T(8,128)(2,1)} %copy.10, pred[1024]{0:T(1024)(128)(4,1)S(1)} %iota_compare_fusion), kind=kOutput, calls=%fused_computation.20 | convolution fusion | flops 8617197568 | bytes 31458304 | tf_op jit(solution)/shard_map/dot_general | solution.py:21
  157.9 19.5 %fusion.3 = (bf16[1,4096,1024]{1,2,0:T(8,128)(2,1)}, bf16[4096,1024]{0,1:T(8,128)(2,1)}) fusion(bf16[4096,1024]{0,1:T(8,128)(2,1)} %copy.9, f32[]{:T(128)S(6)} %rsqrt.3, bf16[1,4096,1024]{1,2,0:T(8,128)(2,1)} %copy.10, bf16[1024,1024]{0,1:T(8,128)(2,1)S(1)} %fusion.14, bf16[1,1024,4096]{2,1,0:T(8,128)(2,1)} %all-gather.3.cloned.1.call-done), kind=kOutput, calls=%fused_computation.6 | convolution fusion | flops 8619294720 | bytes 44040196 | tf_op jit(solution)/shard_map/dot_general | solution.py:28
  177.4 0.0 reduce-scatter.3.cloned.1.call-update
  177.4 0.2 reduce-scatter.5.cloned.1.call-start
  177.7 17.8 %convolution_convert_fusion = bf16[1024,4096]{1,0:T(8,128)(2,1)} fusion(bf16[1024,1024]{0,1:T(8,128)(2,1)S(1)} %fusion.14, bf16[4096,1024]{0,1:T(8,128)(2,1)} %copy.9, bf16[1,4096,1024]{1,2,0:T(8,128)(2,1)} %copy.10), kind=kOutput, calls=%fused_computation.11 | convolution fusion | flops 8610906112 | bytes 27262976 | tf_op jit(solution)/shard_map/dot_general | solution.py:34
  195.5 0.0 reduce-scatter.5.cloned.1.call-update
  195.5 12.1 %copy.12 = bf16[1,4096,1024]{2,1,0:T(8,128)(2,1)} copy(bf16[1,4096,1024]{1,2,0:T(8,128)(2,1)} %get-tuple-element.6) | data formatting | bytes 16777216
  207.6 54.6 %reduce-scatter.3.cloned.1.call-done = bf16[1024,1024]{0,1:T(8,128)(2,1)} async-done(((bf16[4096,1024]{0,1:T(8,128)(2,1)}), bf16[1024,1024]{0,1:T(8,128)(2,1)}) %reduce-scatter.3.cloned.1.call-update) | async-done | bytes 2097168 | tf_op jit(solution)/shard_map/reduce_scatter | solution.py:41
  262.3 4.1 %copy.11 = f32[1024,1024]{1,0:T(8,128)} copy(bf16[1024,1024]{0,1:T(8,128)(2,1)} %reduce-scatter.3.cloned.1.call-done) | data formatting | bytes 6291456
  266.4 88.3 %reduce-scatter.5.cloned.1.call-done = bf16[128,4096]{1,0:T(8,128)(2,1)} async-done(((bf16[1024,4096]{1,0:T(8,128)(2,1)}), bf16[128,4096]{1,0:T(8,128)(2,1)}) %reduce-scatter.5.cloned.1.call-update) | async-done | bytes 1048592 | tf_op jit(solution)/shard_map/reduce_scatter | solution.py:33
  (1 shorter events, 0.0 us)
Async XLA Ops:
  7.2 131.7 %all-gather.3.cloned.1.call-start = ((), (), s32[]{:S(2)}) async-start(), calls=%async_computation.5 | async-start | bytes 9437184 | tf_op jit(solution)/shard_map/all_gather | solution.py:18
  21.3 108.0 %all-to-all-start = ((bf16[8,128,1024]{2,1,0:T(8,128)(2,1)}), bf16[8,128,1024]{2,1,0:T(8,128)(2,1)S(1)}, u32[]{:S(2)}, u32[]{:S(2)}) async-start(bf16[8,128,1024]{2,1,0:T(8,128)(2,1)} %fusion.19), calls=%async_computation | async-start | bytes 4194304 | tf_op jit(solution)/shard_map/all_to_all | solution.py:13
  27.7 234.6 %reduce-scatter.3.cloned.1.call-start = ((), (), s32[]{:S(2)}) async-start(), calls=%async_computation.3 | async-start | bytes 10485760 | tf_op jit(solution)/shard_map/reduce_scatter | solution.py:41
  177.4 177.2 %reduce-scatter.5.cloned.1.call-start = ((), (), s32[]{:S(2)}) async-start(), calls=%async_computation.4 | async-start | bytes 9437184 | tf_op jit(solution)/shard_map/reduce_scatter | solution.py:33
Sparse Core Ops, SparseCore 0:
  9.6 129.2 all-gather.2
  177.6 84.6 reduce-scatter.2
  265.1 89.4 reduce-scatter.4
